TPU v7x, 256 devices: a whole 4x4x8 slice. The times are simulated.
256 devices in a mesh: vocab: 256 (over z, x, y, core).
Axes of the slice: x: 4, y: 4, z: 8, core: 2. Of those that a mesh axis runs over, the one named last changes fastest.
Arguments:
- hidden: bfloat16 [4096, 2560], P('vocab'), may hold values from -3 to 3
- norm_gain: float32 [2560], replicated, may hold values from 0.1 to 1.9
- head: bfloat16 [2560, 73728], P(None, 'vocab'), may hold values from -50 to 50
- token_ids: int32 [4096], P('vocab'), may hold values from 0 to 73447
- req_len: int32 [512], replicated, may hold values from 1 to 8, as said below
- req_owner: int32 [512], replicated, may hold values from 0 to 255, as said below
Outputs:
- logprob: float32 [4096], P('vocab')
- entropy: float32 [4096], P('vocab')
Inputs may be any that keep to these rules, and one draw needn't show every extreme that they name: `req_len`: each device owns exactly 2 requests; the lengths of one device's requests sum to at most 16, and to exactly 16 on some device. `req_owner`: each device index appears exactly 2 times.
All inputs are finite; a program needn't handle non-finite values.
Results may differ from a plain program's by a relative error of at most 0.0037.
Values may be sent and summed in bfloat16 or wider, within the bound.
A program may use at most 128 MiB of HBM per device.

v0:
```python
import jax
import jax.numpy as jnp
from jax import lax
from jax.sharding import PartitionSpec as P

VOCAB_REAL = 73448
EPS = 1e-05
NEG = -1e30


def slice_stats(rows, chosen, head, col_index, real_cols):
    logits = jnp.dot(rows, head, preferred_element_type=jnp.float32) / 10.0
    logits = jnp.where(real_cols[None, :], logits, NEG)
    rowmax = jnp.max(logits, axis=1)
    expo = jnp.where(real_cols[None, :], jnp.exp(logits - rowmax[:, None]), 0.0)
    total = jnp.sum(expo, axis=1)
    weighted = jnp.sum(jnp.where(real_cols[None, :], expo * logits, 0.0), axis=1)
    picked = jnp.sum(jnp.where(col_index[None, :] == chosen[:, None], logits, 0.0), axis=1)
    return (rowmax, total, weighted, picked)


def body(hidden, norm_gain, head, token_ids, req_len, req_owner):
    local_rows = hidden.shape[0]
    columns = head.shape[1]
    me = lax.axis_index("vocab")
    values = hidden.astype(jnp.float32)
    scale = lax.rsqrt(jnp.mean(values * values, axis=-1, keepdims=True) + EPS)
    normed = (values * scale * norm_gain[None, :]).astype(jnp.bfloat16)
    col_index = me * columns + jnp.arange(columns, dtype=jnp.int32)
    real_cols = col_index < VOCAB_REAL
    all_rows, all_ids = (
        lax.all_gather(normed, "vocab", axis=0, tiled=True),
        lax.all_gather(token_ids, "vocab", axis=0, tiled=True),
    )
    stats = slice_stats(all_rows, all_ids, head, col_index, real_cols)
    rowmax, total, weighted, picked = stats

    def own_part(whole):
        return lax.dynamic_slice_in_dim(whole, me * local_rows, local_rows)

    top_full = lax.pmax(rowmax, "vocab")
    factor = jnp.exp(rowmax - top_full)
    sums = lax.psum((total * factor, weighted * factor, picked), "vocab")
    total_all, weighted_all, picked_all = [own_part(item) for item in sums]
    top = own_part(top_full)
    load = jnp.sum(jnp.where(req_owner == me, req_len, 0))
    live = jnp.arange(local_rows, dtype=jnp.int32) < load
    log_total = jnp.log(total_all)
    logprob = jnp.where(live, picked_all - top - log_total, 0.0)
    entropy = jnp.where(live, top + log_total - weighted_all / total_all, 0.0)
    return (logprob, entropy)


def solution(mesh):
    placed = (P("vocab", None), P(), P(None, "vocab"), P("vocab"), P(), P())
    return jax.shard_map(
        body, mesh=mesh, in_specs=placed, out_specs=(P("vocab"), P("vocab")), check_vma=False
    )
```

profile of v0, /device:TPU:1, one launch (start us, length us, event | category | flops | bytes accessed | tf_op | source)
XLA Modules:
  0.0 319.0 jit_solution(3615898307131070533)
XLA Ops:
  7.2 0.0 copy-start
  7.2 0.0 all-gather.2.cloned.1.call-start
  7.2 1.1 fusion.2
  8.4 1.6 fusion.4
  10.0 0.0 all-gather.2.cloned.1.call-update
  10.0 0.9 dynamic-update-slice
  10.9 82.1 %all-reduce = s32[4096]{0:T(1024)S(1)} all-reduce(s32[4096]{0:T(1024)S(1)} %dynamic-update-slice), channel_id=1, replica_groups=mesh['vocab'=256] {'vocab'}, use_global_device_ids=true, to_apply=%add | all-reduce | flops 4096 | bytes 32768
  93.0 1.4 select_reduce_fusion.2
  94.4 52.5 %all-gather.2.cloned.1.call-done = bf16[4096,2560]{1,0:T(8,128)(2,1)} async-done(((bf16[16,2560]{1,0:T(8,128)(2,1)}), bf16[4096,2560]{1,0:T(8,128)(2,1)}) %all-gather.2.cloned.1.call-update) | async-done | bytes 20971536 | tf_op jit(solution)/shard_map/all_gather | solution.py:32
  146.8 0.0 copy-done
  146.8 12.0 %fusion.7 = (f32[4096]{0:T(1024)S(1)}, f32[4096,288]{0,1:T(8,128)}) fusion(bf16[4096,2560]{1,0:T(8,128)(2,1)} %all-gather.2.cloned.1.call-done, bf16[2560,288]{0,1:T(8,128)(2,1)S(1)} %copy-done, pred[288]{0:T(512)(128)(4,1)S(1)} %broadcast_compare_fusion), kind=kOutput, calls=%fused_computation.20 | convolution fusion | flops 6043332608 | bytes 27181344 | tf_op jit(solution)/shard_map/dot_general | solution.py:12
  158.9 74.6 %pmax.7 = f32[4096]{0:T(1024)S(1)} all-reduce(f32[4096]{0:T(1024)S(1)} %get-tuple-element.12), channel_id=1, replica_groups=mesh['vocab'=256] {'vocab'}, use_global_device_ids=true, to_apply=%region_5.6 | all-reduce | flops 4096 | bytes 32768 | tf_op jit(solution)/shard_map/pmax | solution.py:41
  233.5 3.7 %select_reduce_fusion = (f32[4096]{0:T(1024)S(1)}, f32[4096]{0:T(1024)S(1)}, f32[4096]{0:T(1024)S(1)}) fusion(f32[4096,288]{0,1:T(8,128)} %get-tuple-element.13, f32[4096]{0:T(1024)S(1)} %get-tuple-element.12, pred[288]{0:T(512)(128)(4,1)S(1)} %broadcast_compare_fusion, s32[4096]{0:T(1024)S(1)} %all-reduce, s32[288]{0:T(512)S(1)} %iota_add_fusion), kind=kLoop, calls=%fused_computation.2 | loop fusion | flops 10604544 | bytes 4801952 | tf_op jit(solution)/shard_map/reduce_sum | solution.py:17
  237.2 73.8 %all-reduce.1 = (f32[4096]{0:T(1024)S(1)}, f32[4096]{0:T(1024)S(1)}, f32[4096]{0:T(1024)S(1)}) all-reduce(f32[4096]{0:T(1024)S(1)} %get-tuple-element.4, f32[4096]{0:T(1024)S(1)} %get-tuple-element.11, f32[4096]{0:T(1024)S(1)} %get-tuple-element.10), channel_id=1, replica_groups=mesh['vocab'=256] {'vocab'}, use_global_device_ids=true, to_apply=%region_3.4 | all-reduce | flops 12288 | bytes 98304 | tf_op jit(solution)/shard_map/psum | solution.py:43
  311.0 1.2 compare_select_fusion
  (5 shorter events, 0.0 us)
Async XLA Ops:
  7.2 139.7 %copy-start = (bf16[2560,288]{0,1:T(8,128)(2,1)S(1)}, bf16[2560,288]{0,1:T(8,128)(2,1)}, u32[]{:S(2)}) copy-start(bf16[2560,288]{0,1:T(8,128)(2,1)} %param.8) | copy-start | bytes 4423684
  7.2 139.7 %all-gather.2.cloned.1.call-start = ((), (), s32[]{:S(2)}) async-start(), calls=%async_computation | async-start | bytes 21053440 | tf_op jit(solution)/shard_map/all_gather | solution.py:32
Sparse Core Ops, SparseCore 0:
  11.6 135.2 all-gather.1
where the time goes:
time: 320 us; the launch traced here: 319 us
  blocking collectives  230 us (72%)
  waiting for transfers between devices  52.5 us (16%)
  between operations  14.1 us (4%)
  matrix products  12 us (4%)
  other arithmetic  9.06 us (3%)
    unnamed x1, blocking collectives  82.1 us
    pmax x1, blocking collectives, body(): top_full = lax.pmax(rowmax, 'vocab')  74.6 us
    psum x1, blocking collectives, body(): sums = lax.psum((total * factor, weighted * factor, picked), 'vocab')  73.8 us
    all_gather x1, waiting for transfers between devices, body(): lax.all_gather(normed, 'vocab', axis=0, tiled=True)  52.5 us
    dot_general x1, matrix products, slice_stats(): logits = jnp.dot(rows, head, preferred_element_type=jnp.float32) / 10.0  12 us
  transfers between devices with their start and end apart: 1, of which 1 were waited for; matrix products, arithmetic and copies ran while one was open for 1% of the time, Pallas kernels for 0%

commit v1 on v0

--- a/solution.py
+++ b/solution.py
@@ -1,3 +1,4 @@
+import functools
 import jax
 import jax.numpy as jnp
 from jax import lax
@@ -6,6 +7,21 @@
 VOCAB_REAL = 73448
 EPS = 1e-05
 NEG = -1e30
+
+
+def state_the_series_all(content, which_axis):
+    return jnp.concatenate(
+        lax.all_to_all(
+            jnp.stack(tuple((content for _ in range(lax.axis_size(which_axis)))), axis=0),
+            which_axis,
+            split_axis=0,
+            concat_axis=0,
+        ),
+        axis=0,
+    )
+
+
+press_slabs = functools.partial(state_the_series_all, which_axis="vocab")
 
 
 def slice_stats(rows, chosen, head, col_index, real_cols):
@@ -29,7 +45,7 @@
     col_index = me * columns + jnp.arange(columns, dtype=jnp.int32)
     real_cols = col_index < VOCAB_REAL
     all_rows, all_ids = (
-        lax.all_gather(normed, "vocab", axis=0, tiled=True),
+        press_slabs(normed),
         lax.all_gather(token_ids, "vocab", axis=0, tiled=True),
     )
     stats = slice_stats(all_rows, all_ids, head, col_index, real_cols)

time: 320 us -> 691 us (2.16)
  blocking collectives: 230 us -> 645 us
  waiting for transfers between devices: 52.5 us -> 0.01 us
  starting transfers between devices: 0.04 us -> 16.5 us
  between operations: 14.1 us -> 0.71 us
    unnamed x1, blocking collectives: 82.1 us -> 498 us
    all_gather x1 -> x0, waiting for transfers between devices: 52.5 us -> none  [body(): lax.all_gather(normed, 'vocab', axis=0, tiled=True)]
    all_to_all x0 -> x1, starting transfers between devices: none -> 16.5 us  [state_the_series_all(): lax.all_to_all(jnp.stack(tuple((content for _ in range(lax.axis_size(whic...]
    another operation x0 -> x1, local copies, waits for them, and re-layouts: none -> 7.25 us  [state_the_series_all(): jnp.stack(tuple((content for _ in range(lax.axis_size(which_axis)))), axi...]
  transfers between devices with their start and end apart: 1 -> 1, of which waited for: 1 -> 0; matrix products, arithmetic and copies ran while one was open for 1% -> 0% of each run, Pallas kernels for 0% -> 0%
where the time goes in v1:
time: 691 us; the launch traced here: 690 us
  blocking collectives  645 us (93%)
  starting transfers between devices  16.5 us (2%)
  matrix products  12 us (2%)
  other arithmetic  7.57 us (1%)
  local copies, waits for them, and re-layouts  7.55 us (1%)
    unnamed x1, blocking collectives  498 us
    pmax x1, blocking collectives, body(): top_full = lax.pmax(rowmax, 'vocab')  74.4 us
    psum x1, blocking collectives, body(): sums = lax.psum((total * factor, weighted * factor, picked), 'vocab')  73.4 us
    all_to_all x1, starting transfers between devices, state_the_series_all(): lax.all_to_all(jnp.stack(tuple((content for _ in range(lax.axis_size(whic...  16.5 us
  transfers between devices with their start and end apart: 1, of which 0 were waited for; matrix products, arithmetic and copies ran while one was open for 0% of the time, Pallas kernels for 0%

profile of v1, /device:TPU:1, one launch (start us, length us, event | category | flops | bytes accessed | tf_op | source)
XLA Modules:
  0.0 689.9 jit_solution(3392084549813575766)
XLA Ops:
  0.6 0.0 copy-start
  0.6 1.1 fusion.2
  1.8 1.0 fusion.4
  2.8 7.2 %stack.2 = bf16[256,16,2560]{2,1,0:T(8,128)(2,1)} broadcast(bf16[16,2560]{1,0:T(8,128)(2,1)S(1)} %fusion.4), dimensions={1,2} | broadcast | bytes 21053440 | tf_op jit(solution)/shard_map/stack | solution.py:15
  10.0 0.0 copy-start.3
  10.0 0.0 copy-start.1
  10.0 0.0 copy-start.2
  10.0 16.5 %all-to-all-start = ((bf16[256,16,2560]{2,1,0:T(8,128)(2,1)}), bf16[256,16,2560]{2,1,0:T(8,128)(2,1)}, u32[]{:S(2)}, u32[]{:S(2)}) async-start(bf16[256,16,2560]{2,1,0:T(8,128)(2,1)} %stack.2), calls=%async_computation | async-start | bytes 41943040 | tf_op jit(solution)/shard_map/all_to_all | solution.py:14
  26.6 0.0 copy-done.3
  26.6 0.3 dynamic-update-slice
  26.9 497.7 %all-reduce = s32[4096]{0:T(1024)S(1)} all-reduce(s32[4096]{0:T(1024)S(1)} %dynamic-update-slice), channel_id=1, replica_groups=mesh['vocab'=256] {'vocab'}, use_global_device_ids=true, to_apply=%add | all-reduce | flops 4096 | bytes 32768
  524.6 0.0 copy-done.1
  524.6 0.0 copy-done.2
  524.6 0.6 select_reduce_fusion.2
  525.2 0.0 all-to-all-done
  525.2 0.0 copy-done
  525.2 12.0 %fusion.7 = (f32[4096]{0:T(1024)S(1)}, f32[4096,288]{0,1:T(8,128)}) fusion(bf16[4096,2560]{1,0:T(8,128)(2,1)} %bitcast, bf16[2560,288]{0,1:T(8,128)(2,1)S(1)} %copy-done, pred[288]{0:T(512)(128)(4,1)S(1)} %broadcast_compare_fusion), kind=kOutput, calls=%fused_computation.20 | convolution fusion | flops 6043332608 | bytes 27181344 | tf_op jit(solution)/shard_map/dot_general | solution.py:28
  537.2 74.4 %pmax.7 = f32[4096]{0:T(1024)S(1)} all-reduce(f32[4096]{0:T(1024)S(1)} %get-tuple-element.12), channel_id=1, replica_groups=mesh['vocab'=256] {'vocab'}, use_global_device_ids=true, to_apply=%region_5.6 | all-reduce | flops 4096 | bytes 32768 | tf_op jit(solution)/shard_map/pmax | solution.py:57
  611.6 3.7 select_reduce_fusion
  615.3 73.4 %all-reduce.1 = (f32[4096]{0:T(1024)S(1)}, f32[4096]{0:T(1024)S(1)}, f32[4096]{0:T(1024)S(1)}) all-reduce(f32[4096]{0:T(1024)S(1)} %get-tuple-element.4, f32[4096]{0:T(1024)S(1)} %get-tuple-element.11, f32[4096]{0:T(1024)S(1)} %get-tuple-element.10), channel_id=1, replica_groups=mesh['vocab'=256] {'vocab'}, use_global_device_ids=true, to_apply=%region_3.4 | all-reduce | flops 12288 | bytes 98304 | tf_op jit(solution)/shard_map/psum | solution.py:59
  688.7 1.1 compare_select_fusion
  (5 shorter events, 0.0 us)
Async XLA Ops:
  0.6 524.6 %copy-start = (bf16[2560,288]{0,1:T(8,128)(2,1)S(1)}, bf16[2560,288]{0,1:T(8,128)(2,1)}, u32[]{:S(2)}) copy-start(bf16[2560,288]{0,1:T(8,128)(2,1)} %param.8) | copy-start | bytes 4423684
  10.0 16.6 %copy-start.3 = (s32[16]{0:T(128)S(1)}, s32[16]{0:T(128)}, u32[]{:S(2)}) copy-start(s32[16]{0:T(128)} %param.9) | copy-start | bytes 196
  10.0 514.6 %copy-start.1 = (s32[512]{0:T(512)S(1)}, s32[512]{0:T(512)}, u32[]{:S(2)}) copy-start(s32[512]{0:T(512)} %param.10) | copy-start | bytes 6148
  10.0 514.6 %copy-start.2 = (s32[512]{0:T(512)S(1)}, s32[512]{0:T(512)}, u32[]{:S(2)}) copy-start(s32[512]{0:T(512)} %param.11) | copy-start | bytes 6148
  10.0 515.2 %all-to-all-start = ((bf16[256,16,2560]{2,1,0:T(8,128)(2,1)}), bf16[256,16,2560]{2,1,0:T(8,128)(2,1)}, u32[]{:S(2)}, u32[]{:S(2)}) async-start(bf16[256,16,2560]{2,1,0:T(8,128)(2,1)} %stack.2), calls=%async_computation | async-start | bytes 41943040 | tf_op jit(solution)/shard_map/all_to_all | solution.py:14
